TPU v7x, 128 devices: a whole 4x4x4 slice. The times are simulated.
128 devices in a mesh: group: 8 (over y, core), tile: 16 (over x, z).
Axes of the slice: x: 4, y: 4, z: 4, core: 2. Of those that a mesh axis runs over, the one named last changes fastest.
Arguments:
- embeddings: bfloat16 [49152, 768], P(('group', 'tile')), may hold values from -15 to 15
- clusters: int32 [49152], P(('group', 'tile')), may hold values from 0 to 31, as said below
- cluster_owner: int32 [32], replicated, may hold values from 0 to 7, as said below
Outputs:
- neighbours: bfloat16 [49152, 768], P(('group', 'tile'))
- log_mass: float32 [49152], P(('group', 'tile'))
Inputs may be any that keep to these rules, and one draw needn't show every extreme that they name: Among the 384 rows of one device at most 72 belong to clusters of any one group; in every draw one group has exactly 72 rows on every device. `cluster_owner`: each group owns exactly 4 clusters.
All inputs are finite; a program needn't handle non-finite values.
Results may differ from a plain program's by a relative error of at most 0.034.
Values may be sent and summed in bfloat16 or wider, within the bound.
No kernel may reach another device: no remote copies, remote signals or barrier semaphores. Data moves between devices by JAX's collectives and lax.ppermute only.
A program may use at most 128 MiB of HBM per device.

v0:
```python
import math
import jax
import jax.numpy as jnp
from jax import lax
from jax.sharding import PartitionSpec as P

score_scale = 3.0
penalty = 2.0


def block_scores(queries, query_ids, key_rows, key_ids):
    feature_width = queries.shape[1]
    products = lax.dot_general(
        queries, key_rows, (((1,), (1,)), ((), ())), preferred_element_type=jnp.float32
    )
    differs = (query_ids[:, None] != key_ids[None, :]).astype(jnp.float32)
    return products * (score_scale / math.sqrt(feature_width)) - penalty * differs


def partial_terms(scores, usable, key_rows):
    row_peak = jnp.max(jnp.where(usable, scores, 0.0), axis=1)
    weights = jnp.exp(jnp.where(usable, scores - row_peak[:, None], -jnp.inf))
    row_total = jnp.sum(weights, axis=1)
    weighted = jnp.dot(weights.astype(jnp.bfloat16), key_rows, preferred_element_type=jnp.float32)
    return (row_peak, row_total, weighted)


def combine_terms(former, second):
    row_peak = jnp.maximum(former[0], second[0])
    factor_one = jnp.exp(former[0] - row_peak)
    factor_two = jnp.exp(second[0] - row_peak)
    row_total = former[1] * factor_one + second[1] * factor_two
    weighted = second[2] * factor_two[:, None]
    return (row_peak, row_total, weighted)


def per_device(embeddings, clusters, cluster_owner):
    row_count = embeddings.shape[0]
    feature_width = embeddings.shape[1]
    groups_total = lax.axis_size("group")
    capacity = 3 * row_count // (2 * groups_total)
    slot_count = groups_total * capacity
    cluster_total = cluster_owner.shape[0]
    table_hit = clusters[:, None] == jnp.arange(cluster_total, dtype=jnp.int32)[None, :]
    group_of = jnp.sum(jnp.where(table_hit, cluster_owner[None, :], 0), axis=1)
    same_group = group_of[:, None] == group_of[None, :]
    row_index = jnp.arange(row_count, dtype=jnp.int32)
    earlier = row_index[None, :] < row_index[:, None]
    rank_in = jnp.sum(same_group & earlier, axis=1)
    slot_of = group_of * capacity + rank_in
    slot_index = jnp.arange(slot_count, dtype=jnp.int32)
    placing = slot_index[:, None] == slot_of[None, :]
    outgoing = jnp.dot(
        placing.astype(jnp.bfloat16), embeddings, preferred_element_type=jnp.float32
    ).astype(jnp.bfloat16)
    outgoing_ids = jnp.sum(jnp.where(placing, clusters[None, :] + 1, 0), axis=1) - 1
    arrived, arrived_ids = (
        lax.all_to_all(
            outgoing.reshape(groups_total, capacity, feature_width),
            "group",
            split_axis=0,
            concat_axis=0,
            tiled=True,
        ),
        lax.all_to_all(
            outgoing_ids.reshape(groups_total, capacity),
            "group",
            split_axis=0,
            concat_axis=0,
            tiled=True,
        ),
    )
    queries = arrived.reshape(slot_count, feature_width)
    query_ids = arrived_ids.reshape(slot_count)
    start_state = (
        jnp.zeros((slot_count,), jnp.float32),
        jnp.ones((slot_count,), jnp.float32),
        jnp.zeros((slot_count, feature_width), jnp.float32),
    )
    tile_pos = lax.axis_index("tile")
    query_pos = tile_pos * slot_count + jnp.arange(slot_count, dtype=jnp.int32)
    key_rows = lax.all_gather(queries, "tile", axis=0, tiled=True)
    key_ids = lax.all_gather(query_ids, "tile", axis=0, tiled=True)
    key_pos = jnp.arange(key_rows.shape[0], dtype=jnp.int32)
    scores = block_scores(queries, query_ids, key_rows, key_ids)
    usable = (key_ids[None, :] >= 0) & (key_pos[None, :] != query_pos[:, None])
    partials = combine_terms(start_state, partial_terms(scores, usable, key_rows))
    row_peak, row_total, weighted = partials
    lse_slots = row_peak + jnp.log(row_total)
    neighbour_slots = (weighted / row_total[:, None]).astype(jnp.bfloat16)
    back_rows, back_lse = (
        lax.all_to_all(
            neighbour_slots.reshape(groups_total, capacity, feature_width),
            "group",
            split_axis=0,
            concat_axis=0,
            tiled=True,
        ),
        lax.all_to_all(
            lse_slots.reshape(groups_total, capacity).astype(jnp.bfloat16),
            "group",
            split_axis=0,
            concat_axis=0,
            tiled=True,
        ).astype(jnp.float32),
    )
    flat_rows = back_rows.reshape(slot_count, feature_width)
    neighbours = jnp.take(flat_rows, slot_of, axis=0)
    log_mass = jnp.take(back_lse.reshape(slot_count), slot_of, axis=0).astype(jnp.float32)
    return (neighbours, log_mass)


def solution(mesh):
    placed = (P(("group", "tile"), None), P(("group", "tile")), P())
    return jax.shard_map(
        per_device,
        mesh=mesh,
        in_specs=placed,
        out_specs=(P(("group", "tile"), None), P(("group", "tile"))),
        check_vma=False,
    )
```

profile of v0, /device:TPU:1, one launch (start us, length us, event | category | flops | bytes accessed | tf_op | source)
XLA Modules:
  0.0 218.7 jit_solution(13662327656676615391)
XLA Ops:
  7.2 0.0 copy-start
  7.2 0.0 all-gather.2.cloned.1.call-start
  7.2 0.8 select_reduce_fusion.2
  8.1 0.2 convert_reduce_fusion
  8.3 0.7 multiply_add_fusion
  9.0 0.0 copy-done
  9.0 0.6 convolution_convert_fusion
  9.6 19.4 %all_to_all.22 = bf16[8,72,768]{2,1,0:T(8,128)(2,1)} all-to-all(bf16[8,72,768]{2,1,0:T(8,128)(2,1)S(1)} %bitcast.12), channel_id=1, replica_groups=mesh['group'=8,'tile'=16] {'group'}, dimensions={0} | all-to-all | bytes 1769472 | tf_op jit(solution)/shard_map/all_to_all | solution.py:58
  29.0 0.0 all-gather.2.cloned.1.call-update
  29.0 0.2 select_reduce_fusion.1
  29.2 0.7 sub.55
  29.9 4.0 %all-to-all-start = ((s32[8,1,72]{2,1,0:T(1,128)}), s32[8,1,72]{2,1,0:T(1,128)S(1)}, u32[]{:S(2)}, u32[]{:S(2)}) async-start(s32[8,1,72]{2,1,0:T(1,128)} %sub.55), calls=%async_computation | async-start | bytes 8192 | tf_op jit(solution)/shard_map/all_to_all | solution.py:65
  33.9 1.2 dynamic-slice
  35.8 2.6 %all-to-all-done = s32[8,1,72]{2,1,0:T(1,128)S(1)} async-done(((s32[8,1,72]{2,1,0:T(1,128)}), s32[8,1,72]{2,1,0:T(1,128)S(1)}, u32[]{:S(2)}, u32[]{:S(2)}) %all-to-all-start) | async-done | bytes 2336 | tf_op jit(solution)/shard_map/all_to_all | solution.py:65
  38.4 0.5 broadcast.121
  38.9 0.7 reduce.9
  39.6 0.1 reshape.184
  39.7 0.3 dynamic-update-slice
  40.0 63.1 %all-reduce = s32[9216]{0:T(1024)S(1)} all-reduce(s32[9216]{0:T(1024)S(1)} %dynamic-update-slice), channel_id=1, replica_groups=mesh['group'=8,'tile'=16] {'tile'}, use_global_device_ids=true, to_apply=%add | all-reduce | flops 9216 | bytes 73728
  103.1 25.9 %all-gather.2.cloned.1.call-done = bf16[9216,768]{1,0:T(8,128)(2,1)} async-done(((bf16[576,768]{1,0:T(8,128)(2,1)}), bf16[9216,768]{1,0:T(8,128)(2,1)}) %all-gather.2.cloned.1.call-update) | async-done | bytes 14155792 | tf_op jit(solution)/shard_map/all_gather | solution.py:82
  128.9 18.6 %select_reduce_fusion = (f32[576]{0:T(1024)S(1)}, f32[576,9216]{1,0:T(8,128)}) fusion(s32[9216]{0:T(1024)S(1)} %all-reduce, s32[576]{0:T(1024)S(1)} %iota_add_fusion, s32[576]{0:T(1024)S(1)} %reshape.184, pred[9216]{0:T(1024)(128)(4,1)S(1)} %broadcast_compare_fusion, bf16[576,768]{1,0:T(8,128)(2,1)} %bitcast.11, ...), kind=kOutput, calls=%fused_computation.3 | convolution fusion | flops 8196193792 | bytes 36327168 | tf_op jit(solution)/shard_map/dot_general | solution.py:13
  147.6 13.3 %fusion.17 = f32[576]{0:T(1024)S(1)} fusion(f32[576]{0:T(1024)S(1)} %get-tuple-element.6, s32[9216]{0:T(1024)S(1)} %all-reduce, s32[576]{0:T(1024)S(1)} %reshape.184, f32[576,9216]{1,0:T(8,128)} %get-tuple-element.7, s32[576]{0:T(1024)S(1)} %iota_add_fusion, pred[9216]{0:T(1024)(128)(4,1)S(1)} %broadcast_compare_fusion), kind=kLoop, calls=%fused_computation.46 | loop fusion | flops 47775168 | bytes 21288960 | tf_op jit(solution)/shard_map/reduce_sum | solution.py:23
  160.9 0.1 reduce_sum.42
  160.9 0.1 reduce_max.12
  161.0 0.6 copy.5
  161.6 5.0 %all-to-all-start.3 = ((bf16[8,1,72]{2,1,0:T(2,128)(2,1)}), bf16[8,1,72]{2,1,0:T(2,128)(2,1)S(1)}, u32[]{:S(2)}, u32[]{:S(2)}) async-start(bf16[8,1,72]{2,1,0:T(2,128)(2,1)} %copy.5), calls=%async_computation.3 | async-start | bytes 8192 | tf_op jit(solution)/shard_map/all_to_all | solution.py:99
  166.6 24.0 %divide_convert_fusion = bf16[576,768]{1,0:T(8,128)(2,1)} fusion(bf16[9216,768]{1,0:T(8,128)(2,1)} %all-gather.2.cloned.1.call-done, f32[576]{0:T(1024)S(1)} %get-tuple-element.5, f32[576]{0:T(1024)S(1)} %get-tuple-element.4, f32[576,9216]{1,0:T(8,128)} %get-tuple-element.7, f32[576]{0:T(1024)S(1)} %get-tuple-element.6, s32[9216]{0:T(1024)S(1)} %all-reduce, ...), kind=kOutput, calls=%fused_computation.9 | convolution fusion | flops 8202829824 | bytes 36331776 | tf_op jit(solution)/shard_map/dot_general | solution.py:24
  190.6 0.0 all-to-all-done.3
  190.6 4.8 %all-to-all-start.2 = ((bf16[8,72,768]{2,1,0:T(8,128)(2,1)}), bf16[8,72,768]{2,1,0:T(8,128)(2,1)S(1)}, u32[]{:S(2)}, u32[]{:S(2)}) async-start(bf16[8,72,768]{2,1,0:T(8,128)(2,1)} %bitcast.3), calls=%async_computation.2 | async-start | bytes 1769472 | tf_op jit(solution)/shard_map/all_to_all | solution.py:92
  195.5 0.1 reshape.167
  195.5 1.9 gather_fusion.1
  197.4 0.6 broadcast_select_fusion.1
  198.0 10.7 %all-to-all-done.2 = bf16[8,72,768]{2,1,0:T(8,128)(2,1)S(1)} async-done(((bf16[8,72,768]{2,1,0:T(8,128)(2,1)}), bf16[8,72,768]{2,1,0:T(8,128)(2,1)S(1)}, u32[]{:S(2)}, u32[]{:S(2)}) %all-to-all-start.2) | async-done | bytes 884768 | tf_op jit(solution)/shard_map/all_to_all | solution.py:92
  208.8 2.2 gather_fusion
  210.9 0.9 broadcast_select_fusion
  (9 shorter events, 0.1 us)
Async XLA Ops:
  7.2 1.8 copy-start
  7.2 121.8 %all-gather.2.cloned.1.call-start = ((), (), s32[]{:S(2)}) async-start(), calls=%async_computation.4 | async-start | bytes 15040512 | tf_op jit(solution)/shard_map/all_gather | solution.py:82
  29.9 8.6 %all-to-all-start = ((s32[8,1,72]{2,1,0:T(1,128)}), s32[8,1,72]{2,1,0:T(1,128)S(1)}, u32[]{:S(2)}, u32[]{:S(2)}) async-start(s32[8,1,72]{2,1,0:T(1,128)} %sub.55), calls=%async_computation | async-start | bytes 8192 | tf_op jit(solution)/shard_map/all_to_all | solution.py:65
  161.6 29.0 %all-to-all-start.3 = ((bf16[8,1,72]{2,1,0:T(2,128)(2,1)}), bf16[8,1,72]{2,1,0:T(2,128)(2,1)S(1)}, u32[]{:S(2)}, u32[]{:S(2)}) async-start(bf16[8,1,72]{2,1,0:T(2,128)(2,1)} %copy.5), calls=%async_computation.3 | async-start | bytes 8192 | tf_op jit(solution)/shard_map/all_to_all | solution.py:99
  190.6 18.1 %all-to-all-start.2 = ((bf16[8,72,768]{2,1,0:T(8,128)(2,1)}), bf16[8,72,768]{2,1,0:T(8,128)(2,1)S(1)}, u32[]{:S(2)}, u32[]{:S(2)}) async-start(bf16[8,72,768]{2,1,0:T(8,128)(2,1)} %bitcast.3), calls=%async_computation.2 | async-start | bytes 1769472 | tf_op jit(solution)/shard_map/all_to_all | solution.py:92
Sparse Core Ops, SparseCore 0:
  29.1 99.7 all-gather.1
where the time goes:
time: 219 us
  blocking collectives  82.4 us (38%)
  matrix products  43.2 us (20%)
  waiting for transfers between devices  39.3 us (18%)
  other arithmetic  17.5 us (8%)
  between operations  14.8 us (7%)
  starting transfers between devices  13.8 us (6%)
  local copies, waits for them, and re-layouts  7.68 us (4%)
    unnamed x1, blocking collectives  63.1 us
    all_gather x1, waiting for transfers between devices, per_device(): key_rows = lax.all_gather(queries, 'tile', axis=0, tiled=True)  25.9 us
    dot_general x1, matrix products, partial_terms(): jnp.dot(weights.astype(jnp.bfloat16), key_rows, preferred_element_type=jn...  24 us
    all_to_all x1, blocking collectives, per_device(): lax.all_to_all(outgoing.reshape(groups_total, capacity, feature_width), '...  19.4 us
    dot_general x1, matrix products, block_scores(): lax.dot_general(queries, key_rows, (((1,), (1,)), ((), ())), preferred_el...  18.6 us
    reduce_sum x1, other arithmetic, partial_terms(): row_total = jnp.sum(weights, axis=1)  13.3 us
    all_to_all x1, waiting for transfers between devices, per_device(): lax.all_to_all(neighbour_slots.reshape(groups_total, capacity, feature_wi...  10.7 us
    all_to_all x1, starting transfers between devices, per_device(): lax.all_to_all(lse_slots.reshape(groups_total, capacity).astype(jnp.bfloa...  4.97 us
  transfers between devices with their start and end apart: 4, of which 3 were waited for; matrix products, arithmetic and copies ran while one was open for 14% of the time, Pallas kernels for 0%

commit v1 on v0

--- a/solution.py
+++ b/solution.py
@@ -6,6 +6,11 @@
 
 score_scale = 3.0
 penalty = 2.0
+
+
+def all_by_exchange(block, mesh_axis, dim):
+    sent = jnp.stack([block] * lax.axis_size(mesh_axis))
+    return jnp.concatenate(lax.all_to_all(sent, mesh_axis, 0, 0), axis=dim)
 
 
 def block_scores(queries, query_ids, key_rows, key_ids):
@@ -79,7 +84,7 @@
     )
     tile_pos = lax.axis_index("tile")
     query_pos = tile_pos * slot_count + jnp.arange(slot_count, dtype=jnp.int32)
-    key_rows = lax.all_gather(queries, "tile", axis=0, tiled=True)
+    key_rows = all_by_exchange(queries, "tile", 0)
     key_ids = lax.all_gather(query_ids, "tile", axis=0, tiled=True)
     key_pos = jnp.arange(key_rows.shape[0], dtype=jnp.int32)
     scores = block_scores(queries, query_ids, key_rows, key_ids)

time: 219 us -> 425 us (1.94)
  blocking collectives: 82.4 us -> 295 us
  starting transfers between devices: 13.8 us -> 39.1 us
  waiting for transfers between devices: 39.3 us -> 14.6 us
  between operations: 14.8 us -> 1.41 us
  local copies, waits for them, and re-layouts: 7.68 us -> 13.5 us
    unnamed x1, blocking collectives: 63.1 us -> 278 us
    all_gather x1 -> x0, waiting for transfers between devices: 25.9 us -> none  [per_device(): key_rows = lax.all_gather(queries, 'tile', axis=0, tiled=True)]
    all_to_all x1, starting transfers between devices: 4.97 us -> 20.6 us  [per_device(): lax.all_to_all(lse_slots.reshape(groups_total, capacity).astype(jnp.bfloa...]
    all_to_all x0 -> x1, starting transfers between devices: none -> 7.64 us  [all_by_exchange(): return jnp.concatenate(lax.all_to_all(sent, mesh_axis, 0, 0), axis=dim)]
    another operation x0 -> x1, local copies, waits for them, and re-layouts: none -> 6.42 us  [all_by_exchange(): sent = jnp.stack([block] * lax.axis_size(mesh_axis))]
  transfers between devices with their start and end apart: 4 -> 4, of which waited for: 3 -> 2; matrix products, arithmetic and copies ran while one was open for 14% -> 7% of each run, Pallas kernels for 0% -> 0%
where the time goes in v1:
time: 425 us; the launch traced here: 424 us
  blocking collectives  295 us (69%)
  matrix products  43 us (10%)
  starting transfers between devices  39.1 us (9%)
  other arithmetic  17.5 us (4%)
  waiting for transfers between devices  14.6 us (3%)
  local copies, waits for them, and re-layouts  13.5 us (3%)
    unnamed x1, blocking collectives  278 us
    dot_general x1, matrix products, partial_terms(): jnp.dot(weights.astype(jnp.bfloat16), key_rows, preferred_element_type=jn...  24 us
    all_to_all x1, starting transfers between devices, per_device(): lax.all_to_all(lse_slots.reshape(groups_total, capacity).astype(jnp.bfloa...  20.6 us
    dot_general x1, matrix products, block_scores(): lax.dot_general(queries, key_rows, (((1,), (1,)), ((), ())), preferred_el...  18.4 us
    all_to_all x1, blocking collectives, per_device(): lax.all_to_all(outgoing.reshape(groups_total, capacity, feature_width), '...  16.6 us
    reduce_sum x1, other arithmetic, partial_terms(): row_total = jnp.sum(weights, axis=1)  13.3 us
    all_to_all x1, waiting for transfers between devices, per_device(): lax.all_to_all(neighbour_slots.reshape(groups_total, capacity, feature_wi...  10.7 us
  transfers between devices with their start and end apart: 4, of which 2 were waited for; matrix products, arithmetic and copies ran while one was open for 7% of the time, Pallas kernels for 0%

profile of v1, /device:TPU:1, one launch (start us, length us, event | category | flops | bytes accessed | tf_op | source)
XLA Modules:
  0.0 424.0 jit_solution(2864152347406307552)
XLA Ops:
  0.6 0.0 copy-start
  0.6 0.8 select_reduce_fusion.2
  1.5 0.2 convert_reduce_fusion
  1.7 0.7 multiply_add_fusion
  2.4 0.2 select_reduce_fusion.1
  2.6 0.7 sub.55
  3.3 6.0 %all-to-all-start = ((s32[8,1,72]{2,1,0:T(1,128)}), s32[8,1,72]{2,1,0:T(1,128)S(1)}, u32[]{:S(2)}, u32[]{:S(2)}) async-start(s32[8,1,72]{2,1,0:T(1,128)} %sub.55), calls=%async_computation | async-start | bytes 8192 | tf_op jit(solution)/shard_map/all_to_all | solution.py:70
  9.3 0.0 copy-done
  9.3 0.6 convolution_convert_fusion
  9.9 3.9 all-to-all-done
  13.8 16.6 %all_to_all.27 = bf16[8,72,768]{2,1,0:T(8,128)(2,1)S(1)} all-to-all(bf16[8,72,768]{2,1,0:T(8,128)(2,1)S(1)} %bitcast.13), channel_id=1, replica_groups=mesh['group'=8,'tile'=16] {'group'}, dimensions={0} | all-to-all | bytes 1769472 | tf_op jit(solution)/shard_map/all_to_all | solution.py:63
  30.3 0.0 copy-start.1
  30.3 6.4 %stack.3 = bf16[16,576,768]{2,1,0:T(8,128)(2,1)} broadcast(bf16[576,768]{1,0:T(8,128)(2,1)S(1)} %bitcast.11), dimensions={1,2} | broadcast | bytes 15040512 | tf_op jit(solution)/shard_map/stack | solution.py:12
  36.7 7.6 %all-to-all-start.2 = ((bf16[16,576,768]{2,1,0:T(8,128)(2,1)}), bf16[16,576,768]{2,1,0:T(8,128)(2,1)}, u32[]{:S(2)}, u32[]{:S(2)}) async-start(bf16[16,576,768]{2,1,0:T(8,128)(2,1)} %stack.3), calls=%async_computation.2 | async-start | bytes 28311552 | tf_op jit(solution)/shard_map/all_to_all | solution.py:13
  44.4 0.0 copy-done.1
  44.4 0.6 dynamic-slice
  45.7 0.5 broadcast.122
  46.2 0.7 reduce.9
  46.8 0.1 reshape.190
  46.9 0.3 dynamic-update-slice
  47.2 278.4 %all-reduce = s32[9216]{0:T(1024)S(1)} all-reduce(s32[9216]{0:T(1024)S(1)} %dynamic-update-slice), channel_id=1, replica_groups=mesh['group'=8,'tile'=16] {'tile'}, use_global_device_ids=true, to_apply=%add | all-reduce | flops 9216 | bytes 73728
  325.7 0.0 all-to-all-done.2
  325.7 18.4 %select_reduce_fusion = (f32[576]{0:T(1024)S(1)}, f32[576,9216]{1,0:T(8,128)}) fusion(s32[9216]{0:T(1024)S(1)} %all-reduce, s32[576]{0:T(1024)S(1)} %iota_add_fusion, s32[576]{0:T(1024)S(1)} %reshape.190, pred[9216]{0:T(1024)(128)(4,1)S(1)} %broadcast_compare_fusion, bf16[576,768]{1,0:T(8,128)(2,1)S(1)} %bitcast.12, bf16[9216,768]{1,0:T(8,128)(2,1)} %bitcast.3), kind=kOutput, calls=%fused_computation.3 | convolution fusion | flops 8196193792 | bytes 36327168 | tf_op jit(solution)/shard_map/dot_general | solution.py:18
  344.1 13.3 %fusion.17 = f32[576]{0:T(1024)S(1)} fusion(f32[576]{0:T(1024)S(1)} %get-tuple-element.6, s32[9216]{0:T(1024)S(1)} %all-reduce, s32[576]{0:T(1024)S(1)} %reshape.190, f32[576,9216]{1,0:T(8,128)} %get-tuple-element.7, s32[576]{0:T(1024)S(1)} %iota_add_fusion, pred[9216]{0:T(1024)(128)(4,1)S(1)} %broadcast_compare_fusion), kind=kLoop, calls=%fused_computation.46 | loop fusion | flops 47775168 | bytes 21288960 | tf_op jit(solution)/shard_map/reduce_sum | solution.py:28
  357.4 0.1 reduce_sum.42
  357.4 0.1 reduce_max.12
  357.5 0.6 copy.5
  358.2 20.6 %all-to-all-start.4 = ((bf16[8,1,72]{2,1,0:T(2,128)(2,1)}), bf16[8,1,72]{2,1,0:T(2,128)(2,1)S(1)}, u32[]{:S(2)}, u32[]{:S(2)}) async-start(bf16[8,1,72]{2,1,0:T(2,128)(2,1)} %copy.5), calls=%async_computation.4 | async-start | bytes 8192 | tf_op jit(solution)/shard_map/all_to_all | solution.py:104
  378.8 24.0 %divide_convert_fusion = bf16[576,768]{1,0:T(8,128)(2,1)} fusion(bf16[9216,768]{1,0:T(8,128)(2,1)} %bitcast.3, f32[576]{0:T(1024)S(1)} %get-tuple-element.5, f32[576]{0:T(1024)S(1)} %get-tuple-element.4, f32[576,9216]{1,0:T(8,128)} %get-tuple-element.7, f32[576]{0:T(1024)S(1)} %get-tuple-element.6, s32[9216]{0:T(1024)S(1)} %all-reduce, ...), kind=kOutput, calls=%fused_computation.9 | convolution fusion | flops 8202829824 | bytes 36331776 | tf_op jit(solution)/shard_map/dot_general | solution.py:29
  402.7 0.0 all-to-all-done.4
  402.7 4.8 %all-to-all-start.3 = ((bf16[8,72,768]{2,1,0:T(8,128)(2,1)}), bf16[8,72,768]{2,1,0:T(8,128)(2,1)S(1)}, u32[]{:S(2)}, u32[]{:S(2)}) async-start(bf16[8,72,768]{2,1,0:T(8,128)(2,1)} %bitcast.4), calls=%async_computation.3 | async-start | bytes 1769472 | tf_op jit(solution)/shard_map/all_to_all | solution.py:97
  407.6 0.1 reshape.173
  407.7 1.9 gather_fusion.1
  409.6 0.6 broadcast_select_fusion.1
  410.2 10.7 %all-to-all-done.3 = bf16[8,72,768]{2,1,0:T(8,128)(2,1)S(1)} async-done(((bf16[8,72,768]{2,1,0:T(8,128)(2,1)}), bf16[8,72,768]{2,1,0:T(8,128)(2,1)S(1)}, u32[]{:S(2)}, u32[]{:S(2)}) %all-to-all-start.3) | async-done | bytes 884768 | tf_op jit(solution)/shard_map/all_to_all | solution.py:97
  420.9 2.2 gather_fusion
  423.1 0.9 broadcast_select_fusion
  (9 shorter events, 0.1 us)
Async XLA Ops:
  0.6 8.6 %copy-start = (bf16[384,768]{1,0:T(8,128)(2,1)S(1)}, bf16[384,768]{1,0:T(8,128)(2,1)}, u32[]{:S(2)}) copy-start(bf16[384,768]{1,0:T(8,128)(2,1)} %param.3) | copy-start | bytes 1769476
  3.3 10.5 %all-to-all-start = ((s32[8,1,72]{2,1,0:T(1,128)}), s32[8,1,72]{2,1,0:T(1,128)S(1)}, u32[]{:S(2)}, u32[]{:S(2)}) async-start(s32[8,1,72]{2,1,0:T(1,128)} %sub.55), calls=%async_computation | async-start | bytes 8192 | tf_op jit(solution)/shard_map/all_to_all | solution.py:70
  30.3 14.1 %copy-start.1 = (u32[128]{0:T(128)S(1)}, u32[128]{0:T(128)}, u32[]{:S(2)}) copy-start(u32[128]{0:T(128)} %constant.55) | copy-start | bytes 1540
  36.7 288.9 %all-to-all-start.2 = ((bf16[16,576,768]{2,1,0:T(8,128)(2,1)}), bf16[16,576,768]{2,1,0:T(8,128)(2,1)}, u32[]{:S(2)}, u32[]{:S(2)}) async-start(bf16[16,576,768]{2,1,0:T(8,128)(2,1)} %stack.3), calls=%async_computation.2 | async-start | bytes 28311552 | tf_op jit(solution)/shard_map/all_to_all | solution.py:13
  358.2 44.6 %all-to-all-start.4 = ((bf16[8,1,72]{2,1,0:T(2,128)(2,1)}), bf16[8,1,72]{2,1,0:T(2,128)(2,1)S(1)}, u32[]{:S(2)}, u32[]{:S(2)}) async-start(bf16[8,1,72]{2,1,0:T(2,128)(2,1)} %copy.5), calls=%async_computation.4 | async-start | bytes 8192 | tf_op jit(solution)/shard_map/all_to_all | solution.py:104
  402.7 18.2 %all-to-all-start.3 = ((bf16[8,72,768]{2,1,0:T(8,128)(2,1)}), bf16[8,72,768]{2,1,0:T(8,128)(2,1)S(1)}, u32[]{:S(2)}, u32[]{:S(2)}) async-start(bf16[8,72,768]{2,1,0:T(8,128)(2,1)} %bitcast.4), calls=%async_computation.3 | async-start | bytes 1769472 | tf_op jit(solution)/shard_map/all_to_all | solution.py:97
